TPU v7x, 256 devices: a whole 4x4x8 slice. The times are simulated.
256 devices in a mesh: cells: 64 (over x, z, core), cols: 4 (over y).
Axes of the slice: x: 4, y: 4, z: 8, core: 2. Of those that a mesh axis runs over, the one named last changes fastest.
Arguments:
- current: float32 [512, 256, 256], P('cells', 'cols'), may hold values from -6 to 6
- voltage: float32 [512, 256, 256], P('cells', 'cols'), may hold values from -6 to 6
- resistance: float32 [512, 256], P('cells'), may hold values from 0.1 to 1
- elastance: float32 [512, 256], P('cells'), may hold values from 0.1 to 1
- port_gain: float32 [512, 256], P('cells'), may hold values from -6 to 6
- symbols: int32 [3, 256, 256], P(None, 'cells'), may hold values from 0 to 3
- neighbours: int32 [512, 16], P('cells'), may hold values from 0 to 511, as said below
- live_counts: int32 [512], P('cells'), may hold values from 1 to 16, as said below
- membership: int32 [512, 1], P('cells'), may hold values from 0 to 15
- inductance_near: bfloat16 [512, 16, 256, 256], P('cells', None, 'cols'), may hold values from -0.09375 to 0.09375
- source_basis: bfloat16 [512, 64, 256], P('cells'), may hold values from -0.0625 to 0.0625
- target_basis: bfloat16 [512, 64, 256], P('cells'), may hold values from -0.75 to 0.75
- translation: bfloat16 [1024, 1024], replicated, may hold values from -0.1875 to 0.1875
Outputs:
- final_current: float32 [512, 256, 256], P('cells', 'cols')
- final_voltage: float32 [512, 256, 256], P('cells', 'cols')
Inputs may be any that keep to these rules, and one draw needn't show every extreme that they name: `neighbours`: entry 0 of block row t is t itself; every entry names a block at most 8 blocks from t. Block row t uses the first live_counts[t] entries of its list. `membership`: every cluster has at least one block.
All inputs are finite; a program needn't handle non-finite values.
Results may differ from a plain program's by a relative error of at most 0.003.
Values may be sent and summed in bfloat16 or wider, within the bound.
A program may use at most 64 MiB of HBM per device.

v0:
```python
import jax
import jax.numpy as jnp
from jax import lax
from jax.sharding import PartitionSpec as P

REACH = 8
CLUSTERS = 16
STEPS = 3


def padded(block, sides, width):
    for axis, dim in sides:
        count = lax.axis_size(axis)
        forward = [(i, i + 1) for i in range(count - 1)]
        backward = [(target, source) for source, target in forward]
        low = lax.ppermute(
            lax.slice_in_dim(block, block.shape[dim] - width, None, axis=dim), axis, forward
        )
        high = lax.ppermute(lax.slice_in_dim(block, 0, width, axis=dim), axis, backward)
        block = jnp.concatenate([low, block, high], axis=dim)
    return block


def near_field(excite_cols, neighbours, live_counts, inductance_near, anchor):
    block_count, list_length = neighbours.shape
    extended = padded(excite_cols, (("cells", 0),), REACH)
    local_index = neighbours - anchor
    live_mask = jnp.arange(list_length, dtype=jnp.int32)[None, :] < live_counts[:, None]
    gathered = extended[local_index]
    masked = jnp.where(live_mask[:, :, None, None], gathered, jnp.zeros((), jnp.bfloat16))
    return lax.dot_general(
        inductance_near,
        masked,
        (((1, 2), (1, 2)), ((0,), (0,))),
        preferred_element_type=jnp.float32,
    )


def cluster_terms(source_rows, excite_rows, onehot):
    coefficients = lax.dot_general(
        source_rows, excite_rows, (((2,), (1,)), ((0,), (0,))), preferred_element_type=jnp.float32
    )
    return jnp.einsum("gb,bks->gks", onehot, coefficients, precision=lax.Precision.HIGHEST)


def far_field(totals, translation_wide, onehot, target_rows):
    cluster_count, basis_rank, scenario_count = totals.shape
    translated = jnp.dot(
        translation_wide,
        totals.reshape(cluster_count * basis_rank, scenario_count),
        precision=lax.Precision.HIGHEST,
    )
    chosen = jnp.dot(
        onehot.T,
        translated.reshape(cluster_count, basis_rank * scenario_count),
        precision=lax.Precision.HIGHEST,
    )
    chosen = chosen.reshape(onehot.shape[1], basis_rank, scenario_count)
    return lax.dot_general(
        target_rows.astype(jnp.float32),
        chosen,
        (((1,), (1,)), ((0,), (0,))),
        precision=lax.Precision.HIGHEST,
    )


def per_device(
    current,
    voltage,
    resistance,
    elastance,
    port_gain,
    symbols,
    neighbours,
    live_counts,
    membership,
    inductance_near,
    source_basis,
    target_basis,
    translation,
):
    block_count = neighbours.shape[0]
    column_index = lax.axis_index("cols")
    cell_share = inductance_near.shape[2]
    anchor = lax.axis_index("cells") * block_count - REACH
    onehot = (membership[:, 0][None, :] == jnp.arange(CLUSTERS, dtype=jnp.int32)[:, None]).astype(
        jnp.float32
    )
    levels = jnp.repeat((2 * symbols - 3).astype(jnp.float32) / 3.0, 2, axis=1)
    translation_wide = translation.astype(jnp.float32)
    resist_rows = lax.dynamic_slice_in_dim(resistance, column_index * cell_share, cell_share, 1)
    elast_rows = lax.dynamic_slice_in_dim(elastance, column_index * cell_share, cell_share, 1)
    port_rows = lax.dynamic_slice_in_dim(port_gain, column_index * cell_share, cell_share, 1)
    source_rows = lax.dynamic_slice_in_dim(source_basis, column_index * cell_share, cell_share, 2)
    target_rows = lax.dynamic_slice_in_dim(target_basis, column_index * cell_share, cell_share, 2)
    for marching in range(STEPS):
        excite = (
            port_rows[:, :, None] * levels[marching][:, None, :]
            - resist_rows[:, :, None] * current
            - voltage
        ).astype(jnp.bfloat16)
        near_part = near_field(excite, neighbours, live_counts, inductance_near, anchor)
        near_rows = lax.psum_scatter(near_part, "cols", scatter_dimension=1, tiled=True)
        totals = lax.psum(cluster_terms(source_rows, excite, onehot), ("cells", "cols"))
        far_rows = far_field(totals, translation_wide, onehot, target_rows)
        current = current + near_rows + far_rows
        voltage = voltage + elast_rows[:, :, None] * current
    return (current, voltage)


def solution(mesh):
    placed = (
        P("cells", "cols", None),
        P("cells", "cols", None),
        P("cells", None),
        P("cells", None),
        P("cells", None),
        P(None, "cells", None),
        P("cells", None),
        P("cells"),
        P("cells", None),
        P("cells", None, "cols", None),
        P("cells", None, None),
        P("cells", None, None),
        P(),
    )
    return jax.shard_map(
        per_device,
        mesh=mesh,
        in_specs=placed,
        out_specs=(P("cells", "cols", None), P("cells", "cols", None)),
        check_vma=False,
    )
```

profile of v0, /device:TPU:1, one launch (start us, length us, event | category | flops | bytes accessed | tf_op | source)
XLA Modules:
  0.0 880.1 jit_solution(15052922207443054519)
XLA Ops:
  8.0 0.0 all-reduce.4.cloned.1.call-start
  8.1 0.8 convert_multiply_fusion
  9.0 0.8 constant_dynamic-slice_fusion.1
  9.8 1.4 subtract_convert_fusion.2
  11.2 4.9 collective-permute-start
  16.1 1.9 collective-permute-start.1
  18.0 1.2 fusion.43
  19.2 1.5 fusion.37
  20.7 1.7 copy.51
  22.4 0.0 reduce-scatter.4.cloned.1.call-start
  22.5 0.1 reshape.77
  22.6 0.1 iota_compare_fusion.1
  22.7 1.2 collective-permute-done.1
  23.9 1.0 pad_maximum_fusion
  24.9 2.8 gather_fusion
  27.7 6.4 fusion.12
  34.1 3.0 copy.47
  37.1 0.0 reduce-scatter.4.cloned.1.call-update
  37.2 0.0 all-reduce.6.cloned.1.call-start
  37.2 0.1 constant_dynamic-slice_fusion
  37.3 247.3 %all-reduce.4.cloned.1.call-done = f32[1024,256]{1,0:T(8,128)} async-done(((f32[1024,256]{1,0:T(8,128)}), f32[1024,256]{1,0:T(8,128)}) %all-reduce.4.cloned.1.call-update) | async-done | bytes 1048592 | tf_op jit(solution)/shard_map/psum | solution.py:104
  284.7 5.7 convolution_bitcast_fusion.2
  290.3 2.5 copy.52
  292.9 2.4 reshape.70
  295.3 1.7 fusion.27
  297.0 0.0 reduce-scatter.4.cloned.1.call-done
  297.0 2.8 subtract_convert_fusion.1
  299.8 2.9 collective-permute-start.2
  302.8 2.5 collective-permute-start.3
  305.2 1.2 fusion.41
  306.4 0.9 fusion.34
  307.3 1.7 copy.58
  309.0 0.2 reduce-scatter.6.cloned.1.call-start
  309.2 0.7 copy-done.7
  309.9 0.6 collective-permute-done.3
  310.6 1.2 pad_maximum_fusion.1
  311.8 2.8 gather_fusion.1
  314.5 6.4 fusion.15
  320.9 3.1 copy.55
  324.0 0.0 all-reduce.8.cloned.1.call-start
  324.1 246.0 %all-reduce.6.cloned.1.call-done = f32[1024,256]{1,0:T(8,128)} async-done(((f32[1024,256]{1,0:T(8,128)}), f32[1024,256]{1,0:T(8,128)}) %all-reduce.6.cloned.1.call-update) | async-done | bytes 1048592 | tf_op jit(solution)/shard_map/psum | solution.py:104
  570.1 5.7 convolution_bitcast_fusion.1
  575.8 2.5 copy.59
  578.4 2.4 reshape.72
  580.8 2.5 fusion.24
  583.3 2.9 subtract_convert_fusion
  586.2 2.9 collective-permute-start.4
  589.1 2.4 collective-permute-start.5
  591.5 1.2 fusion.39
  592.7 0.9 fusion.31
  593.6 1.7 copy.65
  595.3 0.3 reduce-scatter.8.cloned.1.call-start
  595.6 0.7 copy-done.8
  596.3 0.6 collective-permute-done.5
  596.9 1.2 pad_maximum_fusion.2
  598.1 2.8 gather_fusion.2
  600.9 6.4 fusion.18
  607.2 3.1 copy.62
  610.4 246.1 %all-reduce.8.cloned.1.call-done = f32[1024,256]{1,0:T(8,128)} async-done(((f32[1024,256]{1,0:T(8,128)}), f32[1024,256]{1,0:T(8,128)}) %all-reduce.8.cloned.1.call-update) | async-done | bytes 1048592 | tf_op jit(solution)/shard_map/psum | solution.py:104
  856.5 5.7 convolution_bitcast_fusion
  862.2 2.5 copy.66
  864.7 2.4 reshape.74
  867.1 2.5 fusion.21
  869.7 3.1 multiply_add_fusion
  (43 shorter events, 0.2 us)
Async XLA Ops:
  8.0 276.7 %copy-start = (bf16[1024,1024]{1,0:T(8,128)(2,1)S(1)}, bf16[1024,1024]{1,0:T(8,128)(2,1)}, u32[]{:S(2)}) copy-start(bf16[1024,1024]{1,0:T(8,128)(2,1)} %param.25) | copy-start | bytes 6291460
  8.0 14.5 %copy-start.10 = (s32[8,16]{1,0:T(8,128)S(1)}, s32[8,16]{1,0:T(8,128)}, u32[]{:S(2)}) copy-start(s32[8,16]{1,0:T(8,128)} %param.19) | copy-start | bytes 1540
  8.0 14.6 %copy-start.12 = (s32[8]{0:T(128)S(1)}, s32[8]{0:T(128)}, u32[]{:S(2)}) copy-start(s32[8]{0:T(128)} %param.20) | copy-start | bytes 100
  8.0 276.6 %all-reduce.4.cloned.1.call-start = ((), (), s32[]{:S(2)}) async-start(), calls=%async_computation.4 | async-start | bytes 2097152 | tf_op jit(solution)/shard_map/psum | solution.py:104
  11.2 11.5 %collective-permute-start = (bf16[8,64,256]{2,1,0:T(8,128)(2,1)S(1)}, bf16[8,64,256]{2,1,0:T(8,128)(2,1)S(1)}, u32[]{:S(2)}, u32[]{:S(2)}) collective-permute-start(bf16[8,64,256]{2,1,0:T(8,128)(2,1)S(1)} %subtract_convert_fusion.2), channel_id=1, source_target_pairs={{0,4},{4,8},{8,12},{12,16},{16,20},{20,24},{24,28},{28,32},{32,36}... | collective-permute-start | bytes 786440 | tf_op jit(solution)/shard_map/ppermute | solution.py:16
  16.1 7.8 collective-permute-start.1
  22.4 274.6 %reduce-scatter.4.cloned.1.call-start = ((), (), s32[]{:S(2)}) async-start(), calls=%async_computation.3 | async-start | bytes 2621440 | tf_op jit(solution)/shard_map/reduce_scatter | solution.py:103
  34.1 3.2 copy-start.11
  37.2 533.0 %all-reduce.6.cloned.1.call-start = ((), (), s32[]{:S(2)}) async-start(), calls=%async_computation.6 | async-start | bytes 2097152 | tf_op jit(solution)/shard_map/psum | solution.py:104
  37.3 258.0 %copy-start.9 = (s32[8,1]{0,1:T(1,128)S(1)}, s32[8,1]{0,1:T(1,128)}, u32[]{:S(2)}) copy-start(s32[8,1]{0,1:T(1,128)} %param.21) | copy-start | bytes 100
  37.3 259.7 %copy-start.1 = (f32[8,64,256]{2,1,0:T(8,128)S(1)}, f32[8,64,256]{2,1,0:T(8,128)}, u32[]{:S(2)}) copy-start(f32[8,64,256]{2,1,0:T(8,128)} %param.14) | copy-start | bytes 1572868
  299.8 9.4 %copy-start.5 = (bf16[8,64,256]{2,1,0:T(8,128)(2,1)}, bf16[8,64,256]{2,1,0:T(8,128)(2,1)S(1)}, u32[]{:S(2)}) copy-start(bf16[8,64,256]{2,1,0:T(8,128)(2,1)S(1)} %get-tuple-element.9) | copy-start | bytes 786436
  299.8 9.4 %collective-permute-start.2 = (bf16[8,64,256]{2,1,0:T(8,128)(2,1)S(1)}, bf16[8,64,256]{2,1,0:T(8,128)(2,1)S(1)}, u32[]{:S(2)}, u32[]{:S(2)}) collective-permute-start(bf16[8,64,256]{2,1,0:T(8,128)(2,1)S(1)} %get-tuple-element.9), channel_id=1, source_target_pairs={{0,4},{4,8},{8,12},{12,16},{16,20},{20,24},{24,28},{28,32},{32,36}... | collective-permute-start | bytes 786440 | tf_op jit(solution)/shard_map/ppermute | solution.py:16
  302.8 7.8 collective-permute-start.3
  309.0 274.3 %reduce-scatter.6.cloned.1.call-start = ((), (), s32[]{:S(2)}) async-start(), calls=%async_computation.5 | async-start | bytes 2621440 | tf_op jit(solution)/shard_map/reduce_scatter | solution.py:103
  309.2 0.7 copy-start.7
  324.0 532.5 %all-reduce.8.cloned.1.call-start = ((), (), s32[]{:S(2)}) async-start(), calls=%async_computation.8 | async-start | bytes 2097152 | tf_op jit(solution)/shard_map/psum | solution.py:104
  324.1 259.2 %copy-start.2 = (f32[8,64,256]{2,1,0:T(8,128)S(1)}, f32[8,64,256]{2,1,0:T(8,128)}, u32[]{:S(2)}) copy-start(f32[8,64,256]{2,1,0:T(8,128)} %get-tuple-element.10) | copy-start | bytes 1572868
  586.2 9.4 %copy-start.4 = (bf16[8,64,256]{2,1,0:T(8,128)(2,1)}, bf16[8,64,256]{2,1,0:T(8,128)(2,1)S(1)}, u32[]{:S(2)}) copy-start(bf16[8,64,256]{2,1,0:T(8,128)(2,1)S(1)} %get-tuple-element.11) | copy-start | bytes 786436
  586.2 9.4 %collective-permute-start.4 = (bf16[8,64,256]{2,1,0:T(8,128)(2,1)S(1)}, bf16[8,64,256]{2,1,0:T(8,128)(2,1)S(1)}, u32[]{:S(2)}, u32[]{:S(2)}) collective-permute-start(bf16[8,64,256]{2,1,0:T(8,128)(2,1)S(1)} %get-tuple-element.11), channel_id=1, source_target_pairs={{0,4},{4,8},{8,12},{12,16},{16,20},{20,24},{24,28},{28,32},{32,36}... | collective-permute-start | bytes 786440 | tf_op jit(solution)/shard_map/ppermute | solution.py:16
  589.1 7.8 collective-permute-start.5
  595.3 274.4 %reduce-scatter.8.cloned.1.call-start = ((), (), s32[]{:S(2)}) async-start(), calls=%async_computation.7 | async-start | bytes 2621440 | tf_op jit(solution)/shard_map/reduce_scatter | solution.py:103
  595.6 0.7 copy-start.8
  610.4 259.3 %copy-start.3 = (f32[8,64,256]{2,1,0:T(8,128)S(1)}, f32[8,64,256]{2,1,0:T(8,128)}, u32[]{:S(2)}) copy-start(f32[8,64,256]{2,1,0:T(8,128)} %get-tuple-element.10) | copy-start | bytes 1572868
  610.4 259.3 %copy-start.6 = (bf16[8,64,256]{2,1,0:T(8,128)(2,1)S(1)}, bf16[8,64,256]{2,1,0:T(8,128)(2,1)}, u32[]{:S(2)}) copy-start(bf16[8,64,256]{2,1,0:T(8,128)(2,1)} %param.24) | copy-start | bytes 786436
Sparse Core Ops, SparseCore 0:
  22.5 262.0 all-reduce.3
  309.1 260.9 all-reduce.5
  595.4 261.0 all-reduce.7
Sparse Core Ops, SparseCore 1:
  37.2 35.3 reduce-scatter.3
  324.1 34.1 reduce-scatter.5
  610.4 34.1 reduce-scatter.7
where the time goes:
time: 882 us; the launch traced here: 880 us
  waiting for transfers between devices  742 us (84%)
  matrix products  58.5 us (7%)
  local copies, waits for them, and re-layouts  39.8 us (5%)
  starting transfers between devices  18.3 us (2%)
  between operations  15.7 us (2%)
    psum x3, waiting for transfers between devices, per_device(): lax.psum(cluster_terms(source_rows, excite, onehot), ('cells', 'cols'))  739 us
    dot_general x3, matrix products, near_field(): lax.dot_general(inductance_near, masked, (((1, 2), (1, 2)), ((0,), (0,)))...  19.2 us
  transfers between devices with their start and end apart: 12, of which 6 were waited for; matrix products, arithmetic and copies ran while one was open for 10% of the time, Pallas kernels for 0%

commit v1 on v0

v1 whole, which is shorter than its diff:
```python
import functools

import jax
import jax.numpy as jnp
from jax import lax
from jax.experimental import pallas as pl
from jax.experimental.pallas import tpu as pltpu
from jax.sharding import PartitionSpec as P

MESH = pl.DeviceIdType.MESH
CLUSTERS = 16
RANK = 64
STEPS = 3
BF = jnp.bfloat16
F32 = jnp.float32
WIDE = CLUSTERS * RANK

ONCE = ("a_raw", "a_t", "t_all", "t_sel", "sb", "tb", "tmp", "w_src", "w_tgt", "cols", "wm", "nown", "obuf", "lsem")
EACH = ("ext", "ext_t", "xq", "ns", "nr", "rs", "rr", "zs", "zr", "tot", "ch")
SEMS = ("halo_s", "halo_r", "y_s", "y_r", "n_s", "n_r", "rs_s", "rs_r", "z_s", "z_r", "ag_s", "ag_r", "c_s", "c_r")


def kernel(xn, zn, yn, *refs):
    (cur_in, volt_in, res, ela, port, sym, pick, gate, a_hbm, sb_hbm, tb_hbm, t_hbm, cur, volt) = refs[:14]
    rest = list(refs[14:])
    s = dict(zip(ONCE, rest[: len(ONCE)]))
    rest = rest[len(ONCE):]
    steps = []
    for n in range(STEPS):
        steps.append(dict(zip(EACH, rest[: len(EACH)])))
        rest = rest[len(EACH):]
    sems = dict(zip(SEMS, rest))

    me = lax.axis_index("cells")
    yy = lax.axis_index("cols")
    core = lax.rem(me, 2)
    zz = lax.rem(me // 2, zn)
    xx = me // (2 * zn)
    count = 2 * xn * zn
    chunk = WIDE // xn
    per_x = chunk // 128
    blocks = 8
    pairs = 4
    share = 64

    def cell(x, z, c):
        return (x * zn + z) * 2 + c

    right, left = lax.rem(me + 1, count), lax.rem(me + count - 1, count)
    xc_offsets = [(dx, dc) for dx in range(xn) for dc in range(2) if (dx, dc) != (0, 0)]

    def xc_peer(dx, dc):
        return lax.rem(xx + dx, xn), lax.rem(core + dc, 2)

    def xc_from(dx, dc):
        return lax.rem(xx + xn - dx, xn), lax.rem(core + 2 - dc, 2)

    def y_peer(d):
        return lax.rem(yy + d, yn)

    def y_from(d):
        return lax.rem(yy + yn - d, yn)

    loads = [
        pltpu.make_async_copy(src, dst, s["lsem"].at[i])
        for i, (src, dst) in enumerate(
            ((sb_hbm, s["sb"]), (a_hbm, s["a_raw"]), (t_hbm, s["t_all"]), (tb_hbm, s["tb"]))
        )
    ]
    for load in loads:
        load.start()

    barrier = pltpu.get_barrier_semaphore()
    greeted = [(right, yy), (left, yy)]
    greeted += [(me, y_peer(d)) for d in range(1, yn)]
    for dx, dc in xc_offsets:
        x, c = xc_peer(dx, dc)
        greeted.append((cell(x, zz, c), yy))
    greeted += [(cell(xx, lax.rem(zz + dz, zn), core), yy) for dz in range(1, zn)]
    for device in greeted:
        pl.semaphore_signal(barrier, inc=1, device_id=device, device_id_type=MESH)

    packed = jnp.concatenate(
        [res[...], ela[...], port[...], jnp.zeros((128 - 3 * blocks, 256), F32)], axis=0
    )
    s["tmp"][...] = jnp.transpose(packed)
    s["cols"][...] = s["tmp"][pl.ds(pl.multiple_of(yy * share, share), share), :]

    def column(kind, b):
        at = kind * blocks + b
        return s["cols"][:, at:at + 1]

    cur[...] = cur_in[...]
    volt[...] = volt_in[...]

    def excite(n):
        k = steps[n]
        for p in range(pairs):
            halves = []
            level = (2 * sym[n, p:p + 1, :] - 3).astype(F32) / 3.0
            for b in (2 * p, 2 * p + 1):
                value = column(2, b) * level - column(0, b) * cur[b] - volt[b]
                value = value.astype(BF)
                k["ext"][8 + b] = value
                halves.append(value.astype(F32))
            turned = jnp.transpose(jnp.concatenate(halves, axis=0)).astype(BF)
            for q in range(yn):
                k["ext_t"][q, p] = turned[q * share:(q + 1) * share, :]

    def remote(src, dst, send, recv, device):
        return pltpu.make_async_remote_copy(
            src_ref=src, dst_ref=dst, send_sem=send, recv_sem=recv, device_id=device, device_id_type=MESH
        )

    sent = []

    def send(*args):
        copy = remote(*args)
        copy.start()
        sent.append(copy)

    def arrive(slot, send_sem, recv_sem):
        remote(slot, slot, send_sem, recv_sem, (me, yy)).wait_recv()

    def send_excite(n):
        k = steps[n]
        for d in range(1, yn):
            to = y_peer(d)
            send(k["ext_t"].at[to], k["xq"].at[yy], sems["y_s"].at[n, d], sems["y_r"].at[n, d], (me, to))
        own = k["ext"].at[8:16]
        send(own, k["ext"].at[0:8], sems["halo_s"].at[n, 0], sems["halo_r"].at[n, 0], (right, yy))
        send(own, k["ext"].at[16:24], sems["halo_s"].at[n, 1], sems["halo_r"].at[n, 1], (left, yy))
        k["xq"][yy] = k["ext_t"][yy]

    lane = lax.broadcasted_iota(jnp.int32, (1, 128), 1)
    low_lanes = lane < 64

    def prepare():
        loads[0].wait()
        for p in range(pairs):
            both = jnp.concatenate([s["sb"][2 * p], s["sb"][2 * p + 1]], axis=0).astype(F32)
            turned = jnp.transpose(both)
            for y in range(yn):
                part = turned[y * share:(y + 1) * share, :]
                s["w_src"][p, y * 128:y * 128 + 64, :] = jnp.where(low_lanes, part, 0.0).astype(BF)
                s["w_src"][p, y * 128 + 64:y * 128 + 128, :] = jnp.where(low_lanes, 0.0, part).astype(BF)
        for p in range(pairs):
            for q in range(CLUSTERS // 2):
                def hit(b, g):
                    return gate[b, 16 + g]
                first, second = 2 * p, 2 * p + 1
                at = (p * (CLUSTERS // 2) + q) * 2
                s["wm"][at:at + 1, :] = jnp.where(low_lanes, hit(first, 2 * q), hit(second, 2 * q + 1))
                s["wm"][at + 1:at + 2, :] = jnp.where(low_lanes, hit(second, 2 * q), hit(first, 2 * q + 1))
        loads[1].wait()

        def turn(t, carry):
            for jp in range(8):
                halves = []
                for j in (2 * jp, 2 * jp + 1):
                    halves.append(s["a_raw"][t, j].astype(F32) * gate[t, j])
                both = jnp.concatenate(halves, axis=0)
                s["a_t"][t, :, jp * 128:(jp + 1) * 128] = jnp.transpose(both).astype(BF)
            return carry

        lax.fori_loop(0, blocks, turn, 0)
        loads[2].wait()
        for b in range(blocks):
            s["t_sel"][b * RANK:(b + 1) * RANK, :] = s["t_all"][pick[b, 16]]
        loads[3].wait()
        for p in range(pairs):
            both = jnp.concatenate([s["tb"][2 * p], s["tb"][2 * p + 1]], axis=0).astype(F32)
            s["tmp"][...] = jnp.transpose(both)
            part = s["tmp"][pl.ds(pl.multiple_of(yy * share, share), share), :]
            s["w_tgt"][p, 0:64, :] = jnp.where(low_lanes, part, 0.0).astype(BF)
            s["w_tgt"][p, 64:128, :] = jnp.where(low_lanes, 0.0, part).astype(BF)

    for n in range(STEPS):
        k = steps[n]
        if n == 0:
            excite(0)
            pl.semaphore_wait(barrier, len(greeted))
        send_excite(n)
        if n == 0:
            prepare()
        for d in range(1, yn):
            arrive(k["xq"].at[y_from(d)], sems["y_s"].at[n, d], sems["y_r"].at[n, d])
        straight, rolled = [], []
        for p in range(pairs):
            row = jnp.concatenate([k["xq"][y, p] for y in range(yn)], axis=1)
            c = jnp.dot(row, s["w_src"][p], preferred_element_type=F32)
            straight.append(c)
            rolled.append(pltpu.roll(c, 64, 1))
        for q in range(CLUSTERS // 2):
            total = None
            for p in range(pairs):
                at = (p * (CLUSTERS // 2) + q) * 2
                term = straight[p] * s["wm"][at:at + 1, :] + rolled[p] * s["wm"][at + 1:at + 2, :]
                total = term if total is None else total + term
            xq, lq = q // per_x, q % per_x
            for c in range(2):
                k["rs"][xq, c, :, lq * 128:(lq + 1) * 128] = total[c * 32:(c + 1) * 32, :]
        for e, (dx, dc) in enumerate(xc_offsets):
            x, c = xc_peer(dx, dc)
            send(k["rs"].at[x, c], k["rr"].at[e], sems["rs_s"].at[n, e], sems["rs_r"].at[n, e], (cell(x, zz, c), yy))

        arrive(k["ext"].at[0:8], sems["halo_s"].at[n, 0], sems["halo_r"].at[n, 0])
        arrive(k["ext"].at[16:24], sems["halo_s"].at[n, 1], sems["halo_r"].at[n, 1])

        def near_block(t, carry):
            gathered = jnp.concatenate([k["ext"][pick[t, j]] for j in range(16)], axis=0)
            out = jnp.dot(s["a_t"][t], gathered, preferred_element_type=F32)
            s["obuf"][...] = out
            for y in range(yn):
                k["ns"][y, t] = out[y * share:(y + 1) * share, :].astype(BF)
            s["nown"][t] = s["obuf"][pl.ds(pl.multiple_of(yy * share, share), share), :]
            return carry

        for half in range(2):
            lax.fori_loop(half * 4, half * 4 + 4, near_block, 0)
            part = pl.ds(half * 4, 4)
            for d in range(1, yn):
                to = y_peer(d)
                send(
                    k["ns"].at[to, part],
                    k["nr"].at[d - 1, part],
                    sems["n_s"].at[n, half, d],
                    sems["n_r"].at[n, half, d],
                    (me, to),
                )

        total = k["rs"][xx, core]
        for e in range(len(xc_offsets)):
            arrive(k["rr"].at[e], sems["rs_s"].at[n, e], sems["rs_r"].at[n, e])
            total = total + k["rr"][e]
        k["zs"][...] = total
        for dz in range(1, zn):
            send(
                k["zs"],
                k["zr"].at[dz - 1],
                sems["z_s"].at[n, dz],
                sems["z_r"].at[n, dz],
                (cell(xx, lax.rem(zz + dz, zn), core), yy),
            )
        for dz in range(1, zn):
            arrive(k["zr"].at[dz - 1], sems["z_s"].at[n, dz], sems["z_r"].at[n, dz])
            total = total + k["zr"][dz - 1]

        def rows_of(c):
            return pl.ds(pl.multiple_of(c * 32, 32), 32)

        k["tot"][xx, rows_of(core), :] = total
        own = k["tot"].at[xx, rows_of(core)]
        for e, (dx, dc) in enumerate(xc_offsets):
            x, c = xc_peer(dx, dc)
            send(own, own, sems["ag_s"].at[n, e], sems["ag_r"].at[n, e], (cell(x, zz, c), yy))
        for e, (dx, dc) in enumerate(xc_offsets):
            x, c = xc_from(dx, dc)
            arrive(k["tot"].at[x, rows_of(c)], sems["ag_s"].at[n, e], sems["ag_r"].at[n, e])

        full = jnp.concatenate([k["tot"][x] for x in range(xn)], axis=1)
        high = full.astype(BF)
        low = (full - high.astype(F32)).astype(BF)
        both = lax.dot_general(
            jnp.concatenate([high, low], axis=0),
            s["t_sel"][...],
            (((1,), (1,)), ((), ())),
            preferred_element_type=F32,
        )
        k["ch"][yy] = (both[:64] + both[64:]).astype(BF)
        own = k["ch"].at[yy]
        for d in range(1, yn):
            send(own, own, sems["c_s"].at[n, d], sems["c_r"].at[n, d], (me, y_peer(d)))

        for half in range(2):
            part = pl.ds(half * 4, 4)
            for d in range(1, yn):
                arrive(k["nr"].at[d - 1, part], sems["n_s"].at[n, half, d], sems["n_r"].at[n, half, d])
        for b in range(blocks):
            near = s["nown"][b]
            for d in range(1, yn):
                near = near + k["nr"][d - 1, b].astype(F32)
            cur[b] = cur[b] + near
        for d in range(1, yn):
            arrive(k["ch"].at[y_from(d)], sems["c_s"].at[n, d], sems["c_r"].at[n, d])
        for p in range(pairs):
            picked = jnp.concatenate([k["ch"][y, :, p * 128:(p + 1) * 128] for y in range(yn)], axis=0)
            far = lax.dot_general(
                s["w_tgt"][p], picked, (((1,), (1,)), ((), ())), preferred_element_type=F32
            )
            for i in range(2):
                b = 2 * p + i
                now = cur[b] + far[i * 64:(i + 1) * 64, :]
                cur[b] = now
                volt[b] = volt[b] + column(1, b) * now
        if n + 1 < STEPS:
            excite(n + 1)

    for copy in sent:
        copy.wait_send()


def solution(mesh):
    cells, yn = mesh.shape["cells"], mesh.shape["cols"]
    xn = 4 if cells == 64 else 2
    zn = cells // (2 * xn)
    chunk = WIDE // xn
    peers = 2 * xn - 1
    vmem, dma = pltpu.VMEM, pltpu.SemaphoreType.DMA
    once = [
        vmem((8, 16, 64, 256), BF),
        vmem((8, 256, 1024), BF),
        vmem((CLUSTERS, RANK, WIDE), BF),
        vmem((8 * RANK, WIDE), BF),
        vmem((8, RANK, 256), BF),
        vmem((8, RANK, 256), BF),
        vmem((256, 128), F32),
        vmem((4, 512, 128), BF),
        vmem((4, 128, 128), BF),
        vmem((64, 128), F32),
        vmem((64, 128), F32),
        vmem((8, 64, 256), F32),
        vmem((256, 256), F32),
        dma((4,)),
    ]
    each = [
        vmem((24, 64, 256), BF),
        vmem((yn, 4, 64, 128), BF),
        vmem((yn, 4, 64, 128), BF),
        vmem((yn, 8, 64, 256), BF),
        vmem((yn - 1, 8, 64, 256), BF),
        vmem((xn, 2, 32, chunk), F32),
        vmem((peers, 32, chunk), F32),
        vmem((32, chunk), F32),
        vmem((zn - 1, 32, chunk), F32),
        vmem((xn, 64, chunk), F32),
        vmem((yn, 64, 512), BF),
    ]
    sems = [
        dma((STEPS, 2)),
        dma((STEPS, 2)),
        dma((STEPS, yn)),
        dma((STEPS, yn)),
        dma((STEPS, 2, yn)),
        dma((STEPS, 2, yn)),
        dma((STEPS, peers)),
        dma((STEPS, peers)),
        dma((STEPS, zn)),
        dma((STEPS, zn)),
        dma((STEPS, peers)),
        dma((STEPS, peers)),
        dma((STEPS, yn)),
        dma((STEPS, yn)),
    ]
    in_vmem = pl.BlockSpec(memory_space=pltpu.VMEM)
    in_smem = pl.BlockSpec(memory_space=pltpu.SMEM)
    anywhere = pl.BlockSpec(memory_space=pl.ANY)

    def per_device(
        current, voltage, resistance, elastance, port_gain, symbols, neighbours, live_counts, membership, near, sb, tb, trans
    ):
        entry = lax.broadcasted_iota(jnp.int32, (8, 32), 1)
        gate = jnp.where(entry < 16, entry < live_counts[:, None], entry - 16 == membership).astype(F32)
        anchor = lax.axis_index("cells") * 8 - 8
        pick = jnp.concatenate([neighbours - anchor, membership], axis=1)
        args = (
            current, voltage, resistance, elastance, port_gain, symbols, pick, gate, near, sb, tb,
            trans.reshape(CLUSTERS, RANK, WIDE),
        )
        state = jax.ShapeDtypeStruct(current.shape, F32)
        return pl.pallas_call(
            functools.partial(kernel, xn, zn, yn),
            out_shape=(state, state),
            in_specs=[in_vmem] * 6 + [in_smem] * 2 + [anywhere] * 4,
            out_specs=(in_vmem, in_vmem),
            scratch_shapes=once + each * STEPS + sems,
            compiler_params=pltpu.CompilerParams(
                collective_id=0, has_side_effects=True, vmem_limit_bytes=60 * 1024 * 1024
            ),
        )(*args)

    placed = (
        P("cells", "cols", None),
        P("cells", "cols", None),
        P("cells", None),
        P("cells", None),
        P("cells", None),
        P(None, "cells", None),
        P("cells", None),
        P("cells"),
        P("cells", None),
        P("cells", None, "cols", None),
        P("cells", None, None),
        P("cells", None, None),
        P(),
    )
    return jax.shard_map(
        per_device,
        mesh=mesh,
        in_specs=placed,
        out_specs=(P("cells", "cols", None), P("cells", "cols", None)),
        check_vma=False,
    )
```

time: 882 us -> 112 us (0.13)
  waiting for transfers between devices: 742 us -> 0 us
  Pallas kernels: 0 us -> 104 us
  matrix products: 58.5 us -> 0 us
  local copies, waits for them, and re-layouts: 39.8 us -> 4.47 us
  starting transfers between devices: 18.3 us -> 0 us
  between operations: 15.7 us -> 0.66 us
    psum x3 -> x0, waiting for transfers between devices: 739 us -> none  [per_device(): lax.psum(cluster_terms(source_rows, excite, onehot), ('cells', 'cols'))]
    pallas_call x0 -> x1, Pallas kernels: none -> 104 us  [per_device(): pl.pallas_call(functools.partial(kernel, xn, zn, yn), out_shape=(state, s...]
    dot_general x18 -> x0, matrix products: 58.5 us -> none  [the longest x3 19.2 us: near_field(): lax.dot_general(inductance_near, masked, (((1, 2), (1, 2)), ((0,), (0,)))...]
    dot_general x9 -> x0, local copies, waits for them, and re-layouts: 21.8 us -> none  [the longest x3 9.21 us: near_field(): lax.dot_general(inductance_near, masked, (((1, 2), (1, 2)), ((0,), (0,)))...]
    ppermute x6 -> x0, starting transfers between devices: 17.6 us -> none  [the longest x3 10.8 us: padded(): lax.ppermute(lax.slice_in_dim(block, block.shape[dim] - width, None, axis...]
  transfers between devices with their start and end apart: 12 -> 0, of which waited for: 6 -> 0; matrix products, arithmetic and copies ran while one was open for 10% -> 0% of each run, Pallas kernels for 0% -> 0%
where the time goes in v1:
time: 112 us
  Pallas kernels  104 us (93%)
  local copies, waits for them, and re-layouts  4.47 us (4%)
  other arithmetic  2.71 us (2%)
    pallas_call x1, Pallas kernels, per_device(): pl.pallas_call(functools.partial(kernel, xn, zn, yn), out_shape=(state, s...  104 us
    unnamed x3, local copies, waits for them, and re-layouts  4.47 us

profile of v1, /device:TPU:1, one launch (start us, length us, event | category | flops | bytes accessed | tf_op | source)
XLA Modules:
  0.0 111.8 jit_solution(4031068481487681298)
XLA Ops:
  0.7 1.3 %fusion.1.refs_7_ = f32[8,32]{1,0:T(8,128)} fusion(s32[32]{0:T(128)S(1)} %iota_add_fusion, s32[8]{0:T(128)} %param.20, s32[8]{0:T(128)} %bitcast.3, pred[32]{0:T(512)(128)(4,1)S(1)} %iota_compare_fusion.1), kind=kLoop, calls=%fused_computation.3 | loop fusion | flops 1024 | bytes 1248 | tf_op jit(solution)/shard_map/convert_element_type | solution.py:363
  2.0 0.7 broadcast_subtract_fusion
  2.7 0.7 copy.15
  3.4 0.7 pad_add_fusion.refs_6_
  4.1 103.9 %shard_map.140 = (f32[8,64,256]{2,1,0:T(8,128)}, f32[8,64,256]{2,1,0:T(8,128)}) custom-call(f32[8,64,256]{2,1,0:T(8,128)} %refs_0_.1, f32[8,64,256]{2,1,0:T(8,128)} %refs_1_.1, f32[8,256]{1,0:T(8,128)} %refs_2_.1, f32[8,256]{1,0:T(8,128)} %refs_3_.1, f32[8,256]{1,0:T(8,128)} %refs_4_.1, s32[3,4,256]{2,1,0:T(4,128)} %refs_5_.1, s32[8,17]{1,0:T(8,128)} %pad_add_fusion.refs_6_, ...), custom_call_target="tpu_custom_call" | custom-call | tf_op jit(solution)/shard_map/pallas_call | solution.py:371
  108.0 1.9 %copy.18 = f32[8,64,256]{2,1,0:T(8,128)} copy(f32[8,64,256]{2,1,0:T(8,128)} %get-tuple-element.4) | data formatting | bytes 1048576
  109.9 1.9 %copy.19 = f32[8,64,256]{2,1,0:T(8,128)} copy(f32[8,64,256]{2,1,0:T(8,128)} %get-tuple-element.5) | data formatting | bytes 1048576
  (2 shorter events, 0.0 us)

commit v2 on v1

v2 whole, which is shorter than its diff:
```python
import functools

import jax
import jax.numpy as jnp
from jax import lax
from jax.experimental import pallas as pl
from jax.experimental.pallas import tpu as pltpu
from jax.sharding import PartitionSpec as P

MESH = pl.DeviceIdType.MESH
CLUSTERS = 16
RANK = 64
STEPS = 3
PIECES = 2
BF = jnp.bfloat16
F32 = jnp.float32
WIDE = CLUSTERS * RANK

ONCE = ("a_raw", "a_t", "t_all", "t_sel", "sb", "tb", "tmp", "w_src", "w_tgt", "cols", "wm", "nown", "obuf", "lsem")
EACH = ("ext", "ext_t", "xq", "ns", "nr", "rs", "rr", "zs", "zr", "tot", "ch")
SEMS = ("halo_s", "halo_r", "y_s", "y_r", "n_s", "n_r", "rs_s", "rs_r", "z_s", "z_r", "ag_s", "ag_r", "c_s", "c_r")


def kernel(xn, zn, yn, *refs):
    (cur_in, volt_in, res, ela, port, sym, pick, a_hbm, sb_hbm, tb_hbm, t_hbm, cur, volt, last) = refs[:14]
    rest = list(refs[14:])
    s = dict(zip(ONCE, rest[: len(ONCE)]))
    rest = rest[len(ONCE):]
    steps = []
    for n in range(STEPS):
        steps.append(dict(zip(EACH, rest[: len(EACH)])))
        rest = rest[len(EACH):]
    sems = dict(zip(SEMS, rest))

    me = lax.axis_index("cells")
    yy = lax.axis_index("cols")
    core = lax.rem(me, 2)
    zz = lax.rem(me // 2, zn)
    xx = me // (2 * zn)
    count = 2 * xn * zn
    chunk = WIDE // xn
    per_x = chunk // 128
    blocks = 8
    pairs = 4
    share = 64
    piece = share // PIECES
    sub = piece // 2

    def cell(x, z, c):
        return (x * zn + z) * 2 + c

    right, left = lax.rem(me + 1, count), lax.rem(me + count - 1, count)
    xc_offsets = [(dx, dc) for dx in range(xn) for dc in range(2) if (dx, dc) != (0, 0)]

    def xc_peer(dx, dc):
        return lax.rem(xx + dx, xn), lax.rem(core + dc, 2)

    def xc_from(dx, dc):
        return lax.rem(xx + xn - dx, xn), lax.rem(core + 2 - dc, 2)

    def y_peer(d):
        return lax.rem(yy + d, yn)

    def y_from(d):
        return lax.rem(yy + yn - d, yn)

    loads = [
        pltpu.make_async_copy(src, dst, s["lsem"].at[i])
        for i, (src, dst) in enumerate(
            ((sb_hbm, s["sb"]), (a_hbm, s["a_raw"]), (t_hbm, s["t_all"]), (tb_hbm, s["tb"]), (cur_in, cur), (volt_in, volt))
        )
    ]
    for i in (4, 5, 0, 1, 2, 3):
        loads[i].start()

    barrier = pltpu.get_barrier_semaphore()
    greeted = [(right, yy), (left, yy)]
    greeted += [(me, y_peer(d)) for d in range(1, yn)]
    for dx, dc in xc_offsets:
        x, c = xc_peer(dx, dc)
        greeted.append((cell(x, zz, c), yy))
    greeted += [(cell(xx, lax.rem(zz + dz, zn), core), yy) for dz in range(1, zn)]
    for device in greeted:
        pl.semaphore_signal(barrier, inc=1, device_id=device, device_id_type=MESH)

    packed = jnp.concatenate(
        [res[...], ela[...], port[...], jnp.zeros((128 - 3 * blocks, 256), F32)], axis=0
    )
    s["tmp"][...] = jnp.transpose(packed)
    s["cols"][...] = s["tmp"][pl.ds(pl.multiple_of(yy * share, share), share), :]

    def column(kind, b):
        at = kind * blocks + b
        return s["cols"][:, at:at + 1]

    def excite(n):
        k = steps[n]
        for p in range(pairs):
            halves = []
            level = (2 * sym[n, p:p + 1, :] - 3).astype(F32) / 3.0
            for b in (2 * p, 2 * p + 1):
                value = column(2, b) * level - column(0, b) * cur[b] - volt[b]
                value = value.astype(BF)
                k["ext"][8 + b] = value
                halves.append(value.astype(F32))
            turned = jnp.transpose(jnp.concatenate(halves, axis=0)).astype(BF)
            for q in range(yn):
                for h in range(PIECES):
                    at = q * share + h * piece
                    k["ext_t"][q, h, p] = turned[at:at + piece, :]

    def remote(src, dst, send, recv, device):
        return pltpu.make_async_remote_copy(
            src_ref=src, dst_ref=dst, send_sem=send, recv_sem=recv, device_id=device, device_id_type=MESH
        )

    sent = []

    def send(*args):
        copy = remote(*args)
        copy.start()
        sent.append(copy)

    def arrive(slot, send_sem, recv_sem):
        remote(slot, slot, send_sem, recv_sem, (me, yy)).wait_recv()

    def send_excite(n):
        k = steps[n]
        for h in range(PIECES):
            for d in range(1, yn):
                to = y_peer(d)
                send(
                    k["ext_t"].at[to, h], k["xq"].at[yy, h], sems["y_s"].at[n, h, d], sems["y_r"].at[n, h, d], (me, to)
                )
        own = k["ext"].at[8:16]
        send(own, k["ext"].at[0:8], sems["halo_s"].at[n, 0], sems["halo_r"].at[n, 0], (right, yy))
        send(own, k["ext"].at[16:24], sems["halo_s"].at[n, 1], sems["halo_r"].at[n, 1], (left, yy))
        k["xq"][yy] = k["ext_t"][yy]

    lane = lax.broadcasted_iota(jnp.int32, (1, 128), 1)
    low_lanes = lane < 64

    def prepare():
        loads[0].wait()
        for p in range(pairs):
            both = jnp.concatenate([s["sb"][2 * p], s["sb"][2 * p + 1]], axis=0).astype(F32)
            turned = jnp.transpose(both)
            for y in range(yn):
                part = turned[y * share:(y + 1) * share, :]
                s["w_src"][p, y * 128:y * 128 + 64, :] = jnp.where(low_lanes, part, 0.0).astype(BF)
                s["w_src"][p, y * 128 + 64:y * 128 + 128, :] = jnp.where(low_lanes, 0.0, part).astype(BF)
        for p in range(pairs):
            for q in range(CLUSTERS // 2):
                def hit(b, g):
                    return pick[b, 32 + g].astype(F32)
                first, second = 2 * p, 2 * p + 1
                at = (p * (CLUSTERS // 2) + q) * 2
                s["wm"][at:at + 1, :] = jnp.where(low_lanes, hit(first, 2 * q), hit(second, 2 * q + 1))
                s["wm"][at + 1:at + 2, :] = jnp.where(low_lanes, hit(second, 2 * q), hit(first, 2 * q + 1))
        loads[1].wait()

        def turn(t, carry):
            for jp in range(8):
                halves = []
                for j in (2 * jp, 2 * jp + 1):
                    halves.append(s["a_raw"][t, j].astype(F32) * pick[t, 16 + j].astype(F32))
                both = jnp.concatenate(halves, axis=0)
                s["a_t"][t, :, jp * 128:(jp + 1) * 128] = jnp.transpose(both).astype(BF)
            return carry

        lax.fori_loop(0, blocks, turn, 0)
        loads[2].wait()
        for b in range(blocks):
            s["t_sel"][b * RANK:(b + 1) * RANK, :] = s["t_all"][pick[b, 48]]
        loads[3].wait()
        for p in range(pairs):
            both = jnp.concatenate([s["tb"][2 * p], s["tb"][2 * p + 1]], axis=0).astype(F32)
            s["tmp"][...] = jnp.transpose(both)
            part = s["tmp"][pl.ds(pl.multiple_of(yy * share, share), share), :]
            s["w_tgt"][p, 0:64, :] = jnp.where(low_lanes, part, 0.0).astype(BF)
            s["w_tgt"][p, 64:128, :] = jnp.where(low_lanes, 0.0, part).astype(BF)

    for n in range(STEPS):
        k = steps[n]
        if n == 0:
            loads[4].wait()
            loads[5].wait()
            excite(0)
            pl.semaphore_wait(barrier, len(greeted))
        send_excite(n)
        if n == 0:
            prepare()
        for h in range(PIECES):
            for d in range(1, yn):
                arrive(k["xq"].at[y_from(d), h], sems["y_s"].at[n, h, d], sems["y_r"].at[n, h, d])
            straight, rolled = [], []
            for p in range(pairs):
                row = jnp.concatenate([k["xq"][y, h, p] for y in range(yn)], axis=1)
                c = jnp.dot(row, s["w_src"][p], preferred_element_type=F32)
                straight.append(c)
                rolled.append(pltpu.roll(c, 64, 1))
            for q in range(CLUSTERS // 2):
                total = None
                for p in range(pairs):
                    at = (p * (CLUSTERS // 2) + q) * 2
                    term = straight[p] * s["wm"][at:at + 1, :] + rolled[p] * s["wm"][at + 1:at + 2, :]
                    total = term if total is None else total + term
                xq, lq = q // per_x, q % per_x
                for c in range(2):
                    k["rs"][h, xq, c, :, lq * 128:(lq + 1) * 128] = total[c * sub:(c + 1) * sub, :]
            for e, (dx, dc) in enumerate(xc_offsets):
                x, c = xc_peer(dx, dc)
                send(
                    k["rs"].at[h, x, c],
                    k["rr"].at[h, e],
                    sems["rs_s"].at[n, h, e],
                    sems["rs_r"].at[n, h, e],
                    (cell(x, zz, c), yy),
                )

        arrive(k["ext"].at[0:8], sems["halo_s"].at[n, 0], sems["halo_r"].at[n, 0])
        arrive(k["ext"].at[16:24], sems["halo_s"].at[n, 1], sems["halo_r"].at[n, 1])

        def near_block(t, carry):
            gathered = jnp.concatenate([k["ext"][pick[t, j]] for j in range(16)], axis=0)
            out = jnp.dot(s["a_t"][t], gathered, preferred_element_type=F32)
            s["obuf"][...] = out
            for y in range(yn):
                k["ns"][y, t] = out[y * share:(y + 1) * share, :].astype(BF)
            s["nown"][t] = s["obuf"][pl.ds(pl.multiple_of(yy * share, share), share), :]
            return carry

        def near_half(half):
            lax.fori_loop(half * 4, half * 4 + 4, near_block, 0)
            part = pl.ds(half * 4, 4)
            for d in range(1, yn):
                to = y_peer(d)
                send(
                    k["ns"].at[to, part],
                    k["nr"].at[d - 1, part],
                    sems["n_s"].at[n, half, d],
                    sems["n_r"].at[n, half, d],
                    (me, to),
                )

        near_half(0)

        for h in range(PIECES):
            total = k["rs"][h, xx, core]
            for e in range(len(xc_offsets)):
                arrive(k["rr"].at[h, e], sems["rs_s"].at[n, h, e], sems["rs_r"].at[n, h, e])
                total = total + k["rr"][h, e]
            k["zs"][h] = total
            for dz in range(1, zn):
                send(
                    k["zs"].at[h],
                    k["zr"].at[h, dz - 1],
                    sems["z_s"].at[n, h, dz],
                    sems["z_r"].at[n, h, dz],
                    (cell(xx, lax.rem(zz + dz, zn), core), yy),
                )

        near_half(1)

        for h in range(PIECES):
            total = k["zs"][h]
            for dz in range(1, zn):
                arrive(k["zr"].at[h, dz - 1], sems["z_s"].at[n, h, dz], sems["z_r"].at[n, h, dz])
                total = total + k["zr"][h, dz - 1]
            k["tot"][h, xx, core] = total
            own = k["tot"].at[h, xx, core]
            for e, (dx, dc) in enumerate(xc_offsets):
                x, c = xc_peer(dx, dc)
                send(own, own, sems["ag_s"].at[n, h, e], sems["ag_r"].at[n, h, e], (cell(x, zz, c), yy))

        for h in range(PIECES):
            for e, (dx, dc) in enumerate(xc_offsets):
                x, c = xc_from(dx, dc)
                arrive(k["tot"].at[h, x, c], sems["ag_s"].at[n, h, e], sems["ag_r"].at[n, h, e])
            full = jnp.concatenate(
                [jnp.concatenate([k["tot"][h, x, 0], k["tot"][h, x, 1]], axis=0) for x in range(xn)], axis=1
            )
            high = full.astype(BF)
            low = (full - high.astype(F32)).astype(BF)
            both = lax.dot_general(
                jnp.concatenate([high, low], axis=0),
                s["t_sel"][...],
                (((1,), (1,)), ((), ())),
                preferred_element_type=F32,
            )
            k["ch"][yy, h] = (both[:piece] + both[piece:]).astype(BF)
            own = k["ch"].at[yy, h]
            for d in range(1, yn):
                send(own, own, sems["c_s"].at[n, h, d], sems["c_r"].at[n, h, d], (me, y_peer(d)))

        for half in range(2):
            part = pl.ds(half * 4, 4)
            for d in range(1, yn):
                arrive(k["nr"].at[d - 1, part], sems["n_s"].at[n, half, d], sems["n_r"].at[n, half, d])
        for b in range(blocks):
            near = s["nown"][b]
            for d in range(1, yn):
                near = near + k["nr"][d - 1, b].astype(F32)
            cur[b] = cur[b] + near
        for h in range(PIECES):
            for d in range(1, yn):
                arrive(k["ch"].at[y_from(d), h], sems["c_s"].at[n, h, d], sems["c_r"].at[n, h, d])
        for p in range(pairs):
            picked = jnp.concatenate([k["ch"][y, h, :, p * 128:(p + 1) * 128] for y in range(yn) for h in range(PIECES)], axis=0)
            far = lax.dot_general(
                s["w_tgt"][p], picked, (((1,), (1,)), ((), ())), preferred_element_type=F32
            )
            for i in range(2):
                b = 2 * p + i
                if n + 1 == STEPS:
                    last[b] = far[i * 64:(i + 1) * 64, :]
                    continue
                now = cur[b] + far[i * 64:(i + 1) * 64, :]
                cur[b] = now
                volt[b] = volt[b] + column(1, b) * now
        if n + 1 < STEPS:
            excite(n + 1)

    for copy in sent:
        copy.wait_send()


def solution(mesh):
    cells, yn = mesh.shape["cells"], mesh.shape["cols"]
    xn = 4 if cells == 64 else 2
    zn = cells // (2 * xn)
    chunk = WIDE // xn
    piece = 64 // PIECES
    peers = 2 * xn - 1
    vmem, dma = pltpu.VMEM, pltpu.SemaphoreType.DMA
    once = [
        vmem((8, 16, 64, 256), BF),
        vmem((8, 256, 1024), BF),
        vmem((CLUSTERS, RANK, WIDE), BF),
        vmem((8 * RANK, WIDE), BF),
        vmem((8, RANK, 256), BF),
        vmem((8, RANK, 256), BF),
        vmem((256, 128), F32),
        vmem((4, 512, 128), BF),
        vmem((4, 128, 128), BF),
        vmem((64, 128), F32),
        vmem((64, 128), F32),
        vmem((8, 64, 256), F32),
        vmem((256, 256), F32),
        dma((6,)),
    ]
    each = [
        vmem((24, 64, 256), BF),
        vmem((yn, PIECES, 4, piece, 128), BF),
        vmem((yn, PIECES, 4, piece, 128), BF),
        vmem((yn, 8, 64, 256), BF),
        vmem((yn - 1, 8, 64, 256), BF),
        vmem((PIECES, xn, 2, piece // 2, chunk), F32),
        vmem((PIECES, peers, piece // 2, chunk), F32),
        vmem((PIECES, piece // 2, chunk), F32),
        vmem((PIECES, zn - 1, piece // 2, chunk), F32),
        vmem((PIECES, xn, 2, piece // 2, chunk), F32),
        vmem((yn, PIECES, piece, 512), BF),
    ]
    sems = [
        dma((STEPS, 2)),
        dma((STEPS, 2)),
        dma((STEPS, PIECES, yn)),
        dma((STEPS, PIECES, yn)),
        dma((STEPS, 2, yn)),
        dma((STEPS, 2, yn)),
        dma((STEPS, PIECES, peers)),
        dma((STEPS, PIECES, peers)),
        dma((STEPS, PIECES, zn)),
        dma((STEPS, PIECES, zn)),
        dma((STEPS, PIECES, peers)),
        dma((STEPS, PIECES, peers)),
        dma((STEPS, PIECES, yn)),
        dma((STEPS, PIECES, yn)),
    ]
    in_vmem = pl.BlockSpec(memory_space=pltpu.VMEM)
    in_smem = pl.BlockSpec(memory_space=pltpu.SMEM)
    anywhere = pl.BlockSpec(memory_space=pl.ANY)

    def per_device(
        current, voltage, resistance, elastance, port_gain, symbols, neighbours, live_counts, membership, near, sb, tb, trans
    ):
        at = lax.broadcasted_iota(jnp.int32, (8, 64), 1)
        local = jnp.pad(neighbours, ((0, 0), (0, 48))) - (lax.axis_index("cells") * 8 - 8)
        used = (at - 16 < live_counts[:, None]).astype(jnp.int32)
        inside = (at - 32 == membership).astype(jnp.int32)
        pick = jnp.where(at < 16, local, jnp.where(at < 32, used, jnp.where(at < 48, inside, membership)))
        args = (
            current, voltage, resistance, elastance, port_gain, symbols, pick, near, sb, tb,
            trans.reshape(CLUSTERS, RANK, WIDE),
        )
        state = jax.ShapeDtypeStruct(current.shape, F32)
        partial, before, far = pl.pallas_call(
            functools.partial(kernel, xn, zn, yn),
            out_shape=(state, state, state),
            in_specs=[anywhere] * 2 + [in_vmem] * 4 + [in_smem] + [anywhere] * 4,
            out_specs=(in_vmem, in_vmem, in_vmem),
            scratch_shapes=once + each * STEPS + sems,
            compiler_params=pltpu.CompilerParams(
                collective_id=0, has_side_effects=True, vmem_limit_bytes=60 * 1024 * 1024
            ),
        )(*args)
        rows = lax.dynamic_slice_in_dim(elastance, lax.axis_index("cols") * 64, 64, 1)
        after = partial + far
        return after, before + rows[:, :, None] * after

    placed = (
        P("cells", "cols", None),
        P("cells", "cols", None),
        P("cells", None),
        P("cells", None),
        P("cells", None),
        P(None, "cells", None),
        P("cells", None),
        P("cells"),
        P("cells", None),
        P("cells", None, "cols", None),
        P("cells", None, None),
        P("cells", None, None),
        P(),
    )
    return jax.shard_map(
        per_device,
        mesh=mesh,
        in_specs=placed,
        out_specs=(P("cells", "cols", None), P("cells", "cols", None)),
        check_vma=False,
    )
```

time: 112 us -> 100 us (0.89)
  Pallas kernels: 104 us -> 95 us
  local copies, waits for them, and re-layouts: 4.47 us -> 0.76 us
    pallas_call x1, Pallas kernels: 104 us -> 95 us  [per_device(): pl.pallas_call(functools.partial(kernel, xn, zn, yn), out_shape=(state, s...]
    unnamed x3 -> x0, local copies, waits for them, and re-layouts: 4.47 us -> none
    add x0 -> x1, other arithmetic: none -> 2.4 us  [per_device(): return (after, before + rows[:, :, None] * after)]
    select_n x0 -> x1, other arithmetic: none -> 1.38 us  [per_device(): jnp.where(at < 16, local, jnp.where(at < 32, used, jnp.where(at < 48, ins...]
    convert_element_type x1 -> x0, other arithmetic: 1.34 us -> none  [per_device(): jnp.where(entry < 16, entry < live_counts[:, None], entry - 16 == members...]
where the time goes in v2:
time: 100 us
  Pallas kernels  95 us (95%)
  other arithmetic  3.79 us (4%)
    pallas_call x1, Pallas kernels, per_device(): pl.pallas_call(functools.partial(kernel, xn, zn, yn), out_shape=(state, s...  95 us
    add x1, other arithmetic, per_device(): return (after, before + rows[:, :, None] * after)  2.4 us

profile of v2, /device:TPU:1, one launch (start us, length us, event | category | flops | bytes accessed | tf_op | source)
XLA Modules:
  0.0 100.2 jit_solution(13610896969531878684)
XLA Ops:
  0.7 1.4 %select_select_fusion.refs_6_ = s32[8,64]{1,0:T(8,128)} fusion(s32[8,16]{1,0:T(8,128)} %param.19, s32[64]{0:T(128)S(1)} %get-tuple-element.10, s32[64]{0:T(128)S(1)} %get-tuple-element.11, s32[]{:T(128)S(6)} %sub.17, s32[8]{0:T(128)} %bitcast.3, s32[8]{0:T(128)} %param.20, pred[64]{0:T(512)(128)(4,1)S(1)} %get-tuple-element.12, ...), kind=kLoop, calls=%fused_computation.1 | loop fusion | flops 4096 | bytes 3332 | tf_op jit(solution)/shard_map/jit(_where)/select_n | solution.py:392
  2.0 0.8 constant_dynamic-slice_fusion
  2.8 95.0 %shard_map.140 = (f32[8,64,256]{2,1,0:T(8,128)}, f32[8,64,256]{2,1,0:T(8,128)}, f32[8,64,256]{2,1,0:T(8,128)}) custom-call(f32[8,64,256]{2,1,0:T(8,128)} %refs_0_.1, f32[8,64,256]{2,1,0:T(8,128)} %refs_1_.1, f32[8,256]{1,0:T(8,128)} %refs_2_.1, f32[8,256]{1,0:T(8,128)} %refs_3_.1, f32[8,256]{1,0:T(8,128)} %refs_4_.1, s32[3,4,256]{2,1,0:T(4,128)} %refs_5_.1, ...), custom_call_target="tpu_custom_call" | custom-call | tf_op jit(solution)/shard_map/pallas_call | solution.py:398
  97.8 2.4 %multiply_add_fusion = (f32[8,64,256]{2,1,0:T(8,128)}, f32[8,64,256]{2,1,0:T(8,128)}) fusion(f32[8,64,256]{2,1,0:T(8,128)} %get-tuple-element.7, f32[8,64]{1,0:T(8,128)S(1)} %constant_dynamic-slice_fusion, f32[8,64,256]{2,1,0:T(8,128)} %get-tuple-element.5, f32[8,64,256]{2,1,0:T(8,128)} %get-tuple-element.6), kind=kLoop, calls=%fused_computation | loop fusion | flops 393216 | bytes 2623488 | tf_op jit(solution)/shard_map/add | solution.py:410
  (3 shorter events, 0.0 us)
